TPU v7x, 128 devices: a whole 4x4x4 slice. The times are simulated.
128 devices in a mesh: segment: 8 (over z_hi, y), patch: 16 (over x, z_lo, core).
Axes of the slice: x: 4, y: 4, z: 4 (z_hi: 2, z_lo: 2; z = z_hi * 2 + z_lo), core: 2. Of those that a mesh axis runs over, the one named last changes fastest.
Arguments:
- features: bfloat16 [8, 2, 320, 64, 128], P('segment', None, None, 'patch'), may hold values from -48 to 48, as said below
- latent: float32 [2, 4, 64, 128], P(None, None, 'patch'), may hold values from -48 to 48
- plan_pos: int32 [2], replicated, may hold values from 0 to 9
- blocks_used: int32 [8], P('segment'), may hold values from 1 to 2, as said below
- conv1_w: bfloat16 [8, 2, 9, 320, 320], P('segment'), may hold values from -0.109375 to 0.109375
- conv2_w: bfloat16 [8, 2, 9, 320, 320], P('segment'), may hold values from -0.109375 to 0.109375
- norm_gain: float32 [8, 2, 2, 320], P('segment'), may hold values from 0.25 to 1.75
- norm_shift: float32 [8, 2, 2, 320], P('segment'), may hold values from -3 to 3
- in_w: bfloat16 [9, 320, 4], replicated, may hold values from -1 to 1
- head_w: bfloat16 [9, 4, 320], replicated, may hold values from -0.109375 to 0.109375
- head_gain: float32 [320], replicated, may hold values from 0.25 to 1.75
- head_shift: float32 [320], replicated, may hold values from -3 to 3
Outputs:
- latent_out: float32 [2, 4, 64, 128], P(None, None, 'patch', 'segment')
- features_out: bfloat16 [8, 2, 320, 64, 128], P('segment', None, None, 'patch')
Inputs may be any that keep to these rules, and one draw needn't show every extreme that they name: `features`: every entry lies within the range; row magnitudes vary over the rows. `blocks_used`: each section holds 1 or 2 blocks; both counts occur.
All inputs are finite; a program needn't handle non-finite values.
Results may differ from a plain program's by a relative error of at most 0.0075.
Values may be sent and summed in bfloat16 or wider, within the bound.
A program may use at most 64 MiB of HBM per device.

v0:
```python
import jax
import jax.numpy as jnp
from jax import lax
from jax.sharding import PartitionSpec as P
from jax.experimental import pallas as pl
from jax.experimental.pallas import tpu as pltpu

GROUPS = 32
STEPS = 2
SCHED = 12


epsilon = 1e-05
sigma_top = 3.0
sigma_low = 0.1
rho_power = 7.0


def with_halo(block, sides, width):
    for axis, dim in sides:
        count = lax.axis_size(axis)
        forward = [(i, i + 1) for i in range(count - 1)]
        backward = [(target, source) for source, target in forward]
        low = lax.ppermute(
            lax.slice_in_dim(block, block.shape[dim] - width, None, axis=dim), axis, forward
        )
        high = lax.ppermute(lax.slice_in_dim(block, 0, width, axis=dim), axis, backward)
        block = jnp.concatenate([low, block, high], axis=dim)
    return block


def from_behind(shard, axis, by):
    devices = lax.axis_size(axis)
    pairs = [(i, i + by) for i in range(devices) if 0 <= i + by < devices]
    return lax.ppermute(shard, axis, pairs)


def broadcast(shard, axis, root):
    mine = lax.axis_index(axis) == root
    return lax.psum(jnp.where(mine, shard, jnp.zeros_like(shard)), axis)


def sigma_at(position):
    fraction = position.astype(jnp.float32) / (SCHED - 1)
    top_root = sigma_top ** (1.0 / rho_power)
    low_root = sigma_low ** (1.0 / rho_power)
    return (top_root + fraction * (low_root - top_root)) ** rho_power


def exchange_kernel(
    peers, x_ref, top_ref, bot_ref, o_ref, lo_ref, hi_ref, send_sem, recv_sem, row_send, row_recv
):
    me = lax.axis_index("patch")
    seg = lax.axis_index("segment")
    mesh_ids = pl.DeviceIdType.MESH
    barrier = pltpu.get_barrier_semaphore()
    for dist in range(1, peers):
        pl.semaphore_signal(
            barrier, 1, device_id=(seg, lax.rem(me + dist, peers)), device_id_type=mesh_ids
        )
    pl.semaphore_wait(barrier, peers - 1)
    down = pltpu.make_async_remote_copy(
        src_ref=bot_ref,
        dst_ref=lo_ref,
        send_sem=row_send.at[0],
        recv_sem=row_recv.at[0],
        device_id=(seg, jnp.minimum(me + 1, peers - 1)),
        device_id_type=mesh_ids,
    )
    up = pltpu.make_async_remote_copy(
        src_ref=top_ref,
        dst_ref=hi_ref,
        send_sem=row_send.at[1],
        recv_sem=row_recv.at[1],
        device_id=(seg, jnp.maximum(me - 1, 0)),
        device_id_type=mesh_ids,
    )

    @pl.when(me < peers - 1)
    def _():
        down.start()

    @pl.when(me > 0)
    def _():
        up.start()

    copies = []
    for dist in range(1, peers):
        copy = pltpu.make_async_remote_copy(
            src_ref=x_ref,
            dst_ref=o_ref.at[me],
            send_sem=send_sem.at[dist],
            recv_sem=recv_sem.at[dist],
            device_id=(seg, lax.rem(me + dist, peers)),
            device_id_type=mesh_ids,
        )
        copy.start()
        copies.append(copy)
    o_ref[me] = x_ref[...]

    @pl.when(me == 0)
    def _():
        lo_ref[...] = jnp.zeros(lo_ref.shape, lo_ref.dtype)

    @pl.when(me == peers - 1)
    def _():
        hi_ref[...] = jnp.zeros(hi_ref.shape, hi_ref.dtype)

    for copy in copies:
        copy.wait()

    @pl.when(me < peers - 1)
    def _():
        down.wait_send()
        up.wait_recv()

    @pl.when(me > 0)
    def _():
        up.wait_send()
        down.wait_recv()


def exchange_patch(packed, top, bottom):
    peers = lax.axis_size("patch")
    vmem = pl.BlockSpec(memory_space=pltpu.VMEM)
    return pl.pallas_call(
        lambda *refs: exchange_kernel(peers, *refs),
        out_shape=(
            jax.ShapeDtypeStruct((peers,) + packed.shape, packed.dtype),
            jax.ShapeDtypeStruct(top.shape, top.dtype),
            jax.ShapeDtypeStruct(top.shape, top.dtype),
        ),
        in_specs=[vmem] * 3,
        out_specs=(vmem, vmem, vmem),
        scratch_shapes=[
            pltpu.SemaphoreType.DMA((peers,)),
            pltpu.SemaphoreType.DMA((peers,)),
            pltpu.SemaphoreType.DMA((2,)),
            pltpu.SemaphoreType.DMA((2,)),
        ],
        compiler_params=pltpu.CompilerParams(
            collective_id=0 if top.dtype == jnp.bfloat16 else 1, has_side_effects=True
        ),
        name="exchange_stats_rows",
    )(packed, top, bottom)


def group_moments(values, rows):
    batch_size, height, chan_count, col_count = values.shape
    grouped = values.reshape(batch_size, height, GROUPS, chan_count // GROUPS, col_count)
    local_count = chan_count // GROUPS * height * col_count
    peers = lax.axis_size("patch")
    local_sum = jnp.sum(grouped, axis=(1, 3, 4))
    local_center = local_sum / local_count
    local_dev = jnp.sum(
        jnp.square(grouped - local_center[:, None, :, None, None]), axis=(1, 3, 4)
    )
    flat = jnp.concatenate([local_sum.reshape(-1), local_dev.reshape(-1)])
    width = 128 * ((flat.shape[0] + 127) // 128)
    packed = jnp.zeros((8, width), jnp.float32).at[0, : flat.shape[0]].set(flat)
    every, low, high = exchange_patch(packed, rows[:, 0], rows[:, height - 1])
    every = every[:, 0, :]
    half = batch_size * GROUPS
    sums = every[:, :half].reshape(peers, batch_size, GROUPS)
    devs = every[:, half : 2 * half].reshape(peers, batch_size, GROUPS)
    cell_count = local_count * peers
    center = jnp.sum(sums, axis=0) / cell_count
    between = jnp.sum(jnp.square(sums / local_count - center[None]), axis=0) * local_count
    spread = (jnp.sum(devs, axis=0) + between) / cell_count
    return (center, jnp.sqrt(spread + epsilon)), low, high


def act_with_rows(values, rows, gain, shift):
    moments, low, high = group_moments(values, rows)
    full = jnp.concatenate(
        [low[:, None].astype(jnp.float32), values, high[:, None].astype(jnp.float32)], axis=1
    )
    act = norm_silu(full, moments, gain, shift)
    me = lax.axis_index("patch")
    row = lax.broadcasted_iota(jnp.int32, (1, full.shape[1], 1, 1), 1)
    pad = ((row == 0) & (me == 0)) | ((row == full.shape[1] - 1) & (me == lax.axis_size("patch") - 1))
    return jnp.where(pad, 0.0, act).astype(jnp.bfloat16)


def scatter_kernel(count, x_ref, o_ref, send_sem, recv_sem):
    seg = lax.axis_index("segment")
    me = lax.axis_index("patch")
    last = count - 1
    mesh_ids = pl.DeviceIdType.MESH
    barrier = pltpu.get_barrier_semaphore()

    @pl.when(seg == last)
    def _():
        for target in range(last):
            pl.semaphore_signal(barrier, 1, device_id=(target, me), device_id_type=mesh_ids)
        pl.semaphore_wait(barrier, last)
        copies = []
        for target in range(last):
            copy = pltpu.make_async_remote_copy(
                src_ref=x_ref.at[target],
                dst_ref=o_ref,
                send_sem=send_sem.at[target],
                recv_sem=recv_sem.at[0],
                device_id=(target, me),
                device_id_type=mesh_ids,
            )
            copy.start()
            copies.append(copy)
        o_ref[...] = x_ref[last]
        for copy in copies:
            copy.wait_send()

    @pl.when(seg != last)
    def _():
        pl.semaphore_signal(barrier, 1, device_id=(last, me), device_id_type=mesh_ids)
        pl.semaphore_wait(barrier, 1)
        pltpu.make_async_remote_copy(
            src_ref=x_ref.at[0],
            dst_ref=o_ref,
            send_sem=send_sem.at[0],
            recv_sem=recv_sem.at[0],
            device_id=(last, me),
            device_id_type=mesh_ids,
        ).wait_recv()


def scatter_from_last(pieces):
    count = lax.axis_size("segment")
    vmem = pl.BlockSpec(memory_space=pltpu.VMEM)
    return pl.pallas_call(
        lambda *refs: scatter_kernel(count, *refs),
        out_shape=jax.ShapeDtypeStruct(pieces.shape[1:], pieces.dtype),
        in_specs=[vmem],
        out_specs=vmem,
        scratch_shapes=[pltpu.SemaphoreType.DMA((count,)), pltpu.SemaphoreType.DMA((1,))],
        compiler_params=pltpu.CompilerParams(collective_id=2, has_side_effects=True),
        name="scatter_latent_columns",
    )(pieces)


def norm_silu(values, moments, gain, shift):
    center, root_spread = moments
    batch_size, height, chan_count, col_count = values.shape
    grouped = values.reshape(batch_size, height, GROUPS, chan_count // GROUPS, col_count)
    normed = (
        (grouped - center[:, None, :, None, None]) / root_spread[:, None, :, None, None]
    ).reshape(values.shape)
    normed = normed * gain[None, None, :, None] + shift[None, None, :, None]
    return jax.nn.silu(normed)


def conv_kernel(x_ref, w_ref, o_ref):
    batch, rows = o_ref.shape[0], o_ref.shape[1]
    for b in range(batch):
        for r in range(rows):
            acc = None
            for tap in range(9):
                part = jnp.dot(
                    w_ref[tap], x_ref[tap % 3, b, r + tap // 3], preferred_element_type=jnp.float32
                )
                acc = part if acc is None else acc + part
            o_ref[b, r] = acc


def conv_wide(rows_in, weights, block):
    batch, rows_halo, chans, cols = rows_in.shape
    outs = weights.shape[-2]
    padded = jnp.pad(rows_in, ((0, 0), (0, 0), (0, 0), (1, 1)))
    shifted = jnp.stack([padded[..., j : j + cols] for j in range(3)])
    flops = 2 * 9 * batch * (rows_halo - 2) * cols * chans * outs
    out_shape = (batch, rows_halo - 2, outs, cols)
    return pl.pallas_call(
        conv_kernel,
        grid=(1,),
        out_shape=jax.ShapeDtypeStruct(out_shape, jnp.float32),
        in_specs=[
            pl.BlockSpec(shifted.shape, lambda i: (0, 0, 0, 0, 0)),
            pl.BlockSpec((None, None) + weights.shape[2:], lambda i: (0, block, 0, 0, 0)),
        ],
        out_specs=pl.BlockSpec(out_shape, lambda i: (0, 0, 0, 0)),
        cost_estimate=pl.CostEstimate(
            flops=flops,
            transcendentals=0,
            bytes_accessed=shifted.size * 2 + 9 * chans * outs * 2 + batch * (rows_halo - 2) * outs * cols * 4,
        ),
        name="conv3x3_rows",
    )(shifted, weights)


def conv_valid(rows_in, kernel):
    padded = jnp.pad(rows_in, ((0, 0), (0, 0), (0, 0), (1, 1)))
    height = rows_in.shape[1] - 2
    col_count = rows_in.shape[3]
    accum = jnp.zeros((rows_in.shape[0], height, kernel.shape[1], col_count), jnp.float32)
    for tap_no in range(9):
        row_off, col_off = (tap_no // 3, tap_no % 3)
        window = padded[:, row_off : row_off + height, :, col_off : col_off + col_count]
        accum = accum + jnp.einsum(
            "oi,bhiw->bhow", kernel[tap_no], window, preferred_element_type=jnp.float32
        )
    return accum


def resnet_unit(hidden, conv1_w, conv2_w, block, gain_pair, shift_pair):
    hidden_wide = hidden.astype(jnp.float32)
    first_act = act_with_rows(hidden_wide, hidden, gain_pair[0], shift_pair[0])
    middle = conv_wide(first_act, conv1_w, block)
    second = act_with_rows(middle, middle, gain_pair[1], shift_pair[1])
    result = conv_wide(second, conv2_w, block)
    return (hidden_wide + result).astype(jnp.bfloat16)


def head_noise(source, head_w, head_gain, head_shift):
    head_input = act_with_rows(source.astype(jnp.float32), source, head_gain, head_shift)
    return jnp.transpose(conv_valid(head_input, head_w), (0, 2, 1, 3))


def with_rows(values):
    return with_halo(values, (("patch", 1),), 1)


def per_device(
    features,
    latent,
    plan_pos,
    blocks_used,
    conv1_w,
    conv2_w,
    norm_gain,
    norm_shift,
    in_w,
    head_w,
    head_gain,
    head_shift,
):
    segment_count = lax.axis_size("segment")
    segment_pos = lax.axis_index("segment")
    last = segment_count - 1
    current = jnp.transpose(features[0], (0, 2, 1, 3))
    for step_no in range(STEPS):
        arrived = from_behind(current, "segment", 1)
        noise_local = head_noise(current, head_w, head_gain, head_shift)
        position = plan_pos + step_no
        sigma_now = sigma_at(position)
        sigma_next = sigma_at(position + 1)
        latent = latent + (sigma_next - sigma_now)[:, None, None, None] * noise_local
        scaled = (latent / jnp.sqrt(sigma_next * sigma_next + 1.0)[:, None, None, None]).astype(
            jnp.bfloat16
        )
        scaled_first = lax.ppermute(scaled, "segment", [(last, 0)])
        entry_rows = conv_valid(
            with_rows(jnp.transpose(scaled_first, (0, 2, 1, 3))), in_w
        ).astype(jnp.bfloat16)
        source = jnp.where(segment_pos == 0, entry_rows, arrived)
        after_one = resnet_unit(source, conv1_w, conv2_w, 0, norm_gain[0, 0], norm_shift[0, 0])
        current = lax.cond(
            blocks_used[0] >= 2,
            lambda hidden: resnet_unit(
                hidden, conv1_w, conv2_w, 1, norm_gain[0, 1], norm_shift[0, 1]
            ),
            lambda hidden: hidden,
            after_one,
        )
    batch_size, lat_count, height, col_count = latent.shape
    col_share = col_count // segment_count
    latent, current = lax.optimization_barrier((latent, current))
    pieces = latent.reshape(batch_size, lat_count, height, segment_count, col_share)
    pieces = jnp.transpose(pieces, (3, 0, 1, 2, 4)).reshape(segment_count, -1, 128)
    latent_part = scatter_from_last(pieces).reshape(batch_size, lat_count, height, col_share)
    return (latent_part, jnp.transpose(current, (0, 2, 1, 3))[None])


def solution(mesh):
    placed = (
        P("segment", None, None, "patch", None),
        P(None, None, "patch", None),
        P(),
        P("segment"),
        P("segment", None, None, None, None),
        P("segment", None, None, None, None),
        P("segment", None, None, None),
        P("segment", None, None, None),
        P(),
        P(),
        P(),
        P(),
    )
    return jax.shard_map(
        per_device,
        mesh=mesh,
        in_specs=placed,
        out_specs=(P(None, None, "patch", "segment"), P("segment", None, None, "patch", None)),
        check_vma=False,
    )
```

profile of v0, /device:TPU:2, one launch (start us, length us, event | category | flops | bytes accessed | tf_op | source)
XLA Modules:
  0.0 379.5 jit_solution(4722185369608072539)
XLA Ops:
  5.9 11.7 %exchange_stats_rows.14 = (f32[16,8,128]{2,1,0:T(8,128)}, bf16[2,320,128]{2,1,0:T(8,128)(2,1)}, bf16[2,320,128]{2,1,0:T(8,128)(2,1)}) custom-call(f32[8,128]{1,0:T(8,128)} %scatter.36.refs_0_, bf16[2,320,128]{2,1,0:T(8,128)(2,1)} %get-tuple-element.305.refs_1_, bf16[2,320,128]{2,1,0:T(8,128)(2,1)} %get-tuple-element.304.refs_2_), custom_call_target="tpu_custom_call" | custom-call | tf_op jit(solution)/shard_map/exchange_stats_rows/pallas_call | solution.py:126
  26.1 2.9 collective-permute-start.3
  29.0 5.0 %collective-permute-done = bf16[2,4,4,128]{3,1,2,0:T(4,128)(2,1)S(1)} collective-permute-done((bf16[2,4,4,128]{3,1,2,0:T(4,128)(2,1)S(1)}, bf16[2,4,4,128]{3,1,2,0:T(4,128)(2,1)S(1)}, u32[]{:S(2)}, u32[]{:S(2)}) %collective-permute-start) | collective-permute-done | bytes 8224 | tf_op jit(solution)/shard_map/ppermute | solution.py:350
  34.0 1.9 collective-permute-start.1
  35.9 4.5 %collective-permute-start.2 = (bf16[2,1,4,128]{3,2,1,0:T(4,128)(2,1)S(1)}, bf16[2,1,4,128]{3,2,1,0:T(4,128)(2,1)S(1)}, u32[]{:S(2)}, u32[]{:S(2)}) collective-permute-start(bf16[2,1,4,128]{3,2,1,0:T(4,128)(2,1)S(1)} %get-tuple-element.317), channel_id=1, source_target_pairs={{1,0},{2,1},{3,2},{4,3},{5,4},{6,5},{7,6},{8,7},{9,8},{10,9},{11,1... | collective-permute-start | bytes 6152 | tf_op jit(solution)/shard_map/ppermute | solution.py:27
  48.0 10.9 %exchange_stats_rows.15 = (f32[16,8,128]{2,1,0:T(8,128)}, bf16[2,320,128]{2,1,0:T(8,128)(2,1)}, bf16[2,320,128]{2,1,0:T(8,128)(2,1)}) custom-call(f32[8,128]{1,0:T(8,128)} %scatter.37.refs_0_, bf16[2,320,128]{2,1,0:T(8,128)(2,1)} %get-tuple-element.301.refs_1_, bf16[2,320,128]{2,1,0:T(8,128)(2,1)} %get-tuple-element.300.refs_2_), custom_call_target="tpu_custom_call" | custom-call | tf_op jit(solution)/shard_map/exchange_stats_rows/pallas_call | solution.py:126
  65.4 1.9 select_convert_fusion.16
  69.2 1.9 pad_maximum_fusion.4.x_ref
  71.1 8.3 %conv3x3_rows.12 = f32[2,4,320,128]{3,2,1,0:T(8,128)} custom-call(bf16[3,2,6,320,128]{4,3,2,1,0:T(8,128)(2,1)} %pad_maximum_fusion.4.x_ref, bf16[1,2,9,320,320]{4,3,2,1,0:T(8,128)(2,1)} %w_ref.6), custom_call_target="tpu_custom_call" | custom-call | flops 1887436800 | bytes 6103040 | tf_op jit(solution)/shard_map/conv3x3_rows/pallas_call | solution.py:272
  79.4 1.6 reduce_sum.608
  81.3 1.9 slice_bitcast_fusion.12
  84.8 14.6 %exchange_stats_rows.16 = (f32[16,8,128]{2,1,0:T(8,128)}, f32[2,320,128]{2,1,0:T(8,128)}, f32[2,320,128]{2,1,0:T(8,128)}) custom-call(f32[8,128]{1,0:T(8,128)} %scatter.38.refs_0_, f32[2,320,128]{2,1,0:T(8,128)} %get-tuple-element.283.refs_1_, f32[2,320,128]{2,1,0:T(8,128)} %get-tuple-element.282.refs_2_), custom_call_target="tpu_custom_call" | custom-call | tf_op jit(solution)/shard_map/exchange_stats_rows/pallas_call | solution.py:126
  100.9 2.1 select_convert_fusion.14
  105.3 1.9 pad_maximum_fusion.5.x_ref
  107.3 8.3 %conv3x3_rows.13 = f32[2,4,320,128]{3,2,1,0:T(8,128)} custom-call(bf16[3,2,6,320,128]{4,3,2,1,0:T(8,128)(2,1)} %pad_maximum_fusion.5.x_ref, bf16[1,2,9,320,320]{4,3,2,1,0:T(8,128)(2,1)} %w_ref.7), custom_call_target="tpu_custom_call" | custom-call | flops 1887436800 | bytes 6103040 | tf_op jit(solution)/shard_map/conv3x3_rows/pallas_call | solution.py:272
  117.2 6.1 %conditional.2 = (bf16[2,4,320,128]{3,2,1,0:T(8,128)(2,1)S(1)}) conditional(s32[]{:T(128)} %bitcast.85, bf16[2,4,320,128]{3,2,1,0:T(8,128)(2,1)S(1)} %add_convert_fusion.3, (bf16[2,4,320,128]{3,2,1,0:T(8,128)(2,1)S(1)}, f32[1,2,2,320]{3,2,1,0:T(2,128)S(1)}, f32[1,2,2,320]{3,2,1,0:T(2,128)S(1)}, bf16[1,2,9,320,320]{4,3,2,1,0:T(8,128)(2,1)}, ...), branch_computations={%region_21.22_spmd, %region_22.37_spmd} | conditional | flops 3809128960 | bytes 63341760 | solution.py:356
  126.1 10.4 %exchange_stats_rows.17 = (f32[16,8,128]{2,1,0:T(8,128)}, bf16[2,320,128]{2,1,0:T(8,128)(2,1)}, bf16[2,320,128]{2,1,0:T(8,128)(2,1)}) custom-call(f32[8,128]{1,0:T(8,128)} %scatter.41.refs_0_, bf16[2,320,128]{2,1,0:T(8,128)(2,1)} %get-tuple-element.297.refs_1_, bf16[2,320,128]{2,1,0:T(8,128)(2,1)} %get-tuple-element.296.refs_2_), custom_call_target="tpu_custom_call" | custom-call | tf_op jit(solution)/shard_map/exchange_stats_rows/pallas_call | solution.py:126
  143.6 67.0 %collective-permute-done.4 = bf16[2,4,4,128]{3,1,2,0:T(4,128)(2,1)S(1)} collective-permute-done((bf16[2,4,4,128]{3,1,2,0:T(4,128)(2,1)S(1)}, bf16[2,4,4,128]{3,1,2,0:T(4,128)(2,1)S(1)}, u32[]{:S(2)}, u32[]{:S(2)}) %collective-permute-start.4) | collective-permute-done | bytes 8224 | tf_op jit(solution)/shard_map/ppermute | solution.py:350
  210.6 1.9 collective-permute-start.5
  212.5 4.5 %collective-permute-start.6 = (bf16[2,1,4,128]{3,2,1,0:T(4,128)(2,1)S(1)}, bf16[2,1,4,128]{3,2,1,0:T(4,128)(2,1)S(1)}, u32[]{:S(2)}, u32[]{:S(2)}) collective-permute-start(bf16[2,1,4,128]{3,2,1,0:T(4,128)(2,1)S(1)} %get-tuple-element.315), channel_id=1, source_target_pairs={{1,0},{2,1},{3,2},{4,3},{5,4},{6,5},{7,6},{8,7},{9,8},{10,9},{11,1... | collective-permute-start | bytes 6152 | tf_op jit(solution)/shard_map/ppermute | solution.py:27
  221.5 9.1 %collective-permute-done.7 = bf16[2,4,320,128]{3,2,1,0:T(8,128)(2,1)S(1)} collective-permute-done((bf16[2,4,320,128]{3,2,1,0:T(8,128)(2,1)S(1)}, bf16[2,4,320,128]{3,2,1,0:T(8,128)(2,1)S(1)}, u32[]{:S(2)}, u32[]{:S(2)}) %collective-permute-start.7) | collective-permute-done | bytes 655392 | tf_op jit(solution)/shard_map/ppermute | solution.py:35
  233.8 11.0 %exchange_stats_rows.18 = (f32[16,8,128]{2,1,0:T(8,128)}, bf16[2,320,128]{2,1,0:T(8,128)(2,1)}, bf16[2,320,128]{2,1,0:T(8,128)(2,1)}) custom-call(f32[8,128]{1,0:T(8,128)} %scatter.42.refs_0_, bf16[2,320,128]{2,1,0:T(8,128)(2,1)} %get-tuple-element.295.refs_1_, bf16[2,320,128]{2,1,0:T(8,128)(2,1)} %get-tuple-element.294.refs_2_), custom_call_target="tpu_custom_call" | custom-call | tf_op jit(solution)/shard_map/exchange_stats_rows/pallas_call | solution.py:126
  252.0 1.9 pad_maximum_fusion.6.x_ref
  253.9 8.3 %conv3x3_rows.14 = f32[2,4,320,128]{3,2,1,0:T(8,128)} custom-call(bf16[3,2,6,320,128]{4,3,2,1,0:T(8,128)(2,1)} %pad_maximum_fusion.6.x_ref, bf16[1,2,9,320,320]{4,3,2,1,0:T(8,128)(2,1)} %w_ref.6), custom_call_target="tpu_custom_call" | custom-call | flops 1887436800 | bytes 6103040 | tf_op jit(solution)/shard_map/conv3x3_rows/pallas_call | solution.py:272
  262.2 1.6 reduce_sum.635
  264.1 1.9 slice_bitcast_fusion.10
  267.6 14.6 %exchange_stats_rows.19 = (f32[16,8,128]{2,1,0:T(8,128)}, f32[2,320,128]{2,1,0:T(8,128)}, f32[2,320,128]{2,1,0:T(8,128)}) custom-call(f32[8,128]{1,0:T(8,128)} %scatter.43.refs_0_, f32[2,320,128]{2,1,0:T(8,128)} %get-tuple-element.281.refs_1_, f32[2,320,128]{2,1,0:T(8,128)} %get-tuple-element.280.refs_2_), custom_call_target="tpu_custom_call" | custom-call | tf_op jit(solution)/shard_map/exchange_stats_rows/pallas_call | solution.py:126
  283.7 2.1 select_convert_fusion.9
  288.1 1.9 pad_maximum_fusion.7.x_ref
  290.0 8.3 %conv3x3_rows.15 = f32[2,4,320,128]{3,2,1,0:T(8,128)} custom-call(bf16[3,2,6,320,128]{4,3,2,1,0:T(8,128)(2,1)} %pad_maximum_fusion.7.x_ref, bf16[1,2,9,320,320]{4,3,2,1,0:T(8,128)(2,1)} %w_ref.7), custom_call_target="tpu_custom_call" | custom-call | flops 1887436800 | bytes 6103040 | tf_op jit(solution)/shard_map/conv3x3_rows/pallas_call | solution.py:272
  299.9 1.8 conditional.3
  302.6 73.6 %scatter_latent_columns.1 = f32[4,128]{1,0:T(4,128)} custom-call(f32[8,4,128]{2,1,0:T(4,128)} %reshape.1690.refs_0_), custom_call_target="tpu_custom_call" | custom-call | tf_op jit(solution)/shard_map/scatter_latent_columns/pallas_call | solution.py:230
  (295 shorter events, 70.8 us)
Async XLA Ops:
  0.6 3.2 copy-start.4
  3.6 16.6 %copy-start.32 = (f32[320]{0:T(512)S(1)}, f32[320]{0:T(512)}, u32[]{:S(2)}) copy-start(f32[320]{0:T(512)} %param.47) | copy-start | bytes 3844
  3.6 16.6 %copy-start.34 = (f32[320]{0:T(512)S(1)}, f32[320]{0:T(512)}, u32[]{:S(2)}) copy-start(f32[320]{0:T(512)} %param.46) | copy-start | bytes 3844
  19.1 2.3 copy-start.23
  19.1 2.3 copy-start.19
  21.4 1.4 copy-start.38
  22.9 1.7 copy-start.27
  23.7 16.8 %copy-start.28 = (f32[1,2,2,320]{3,2,1,0:T(2,128)S(1)}, f32[1,2,2,320]{3,2,1,0:T(2,128)}, u32[]{:S(2)}) copy-start(f32[1,2,2,320]{3,2,1,0:T(2,128)} %param.43) | copy-start | bytes 15364
  23.7 16.8 %copy-start.30 = (f32[1,2,2,320]{3,2,1,0:T(2,128)S(1)}, f32[1,2,2,320]{3,2,1,0:T(2,128)}, u32[]{:S(2)}) copy-start(f32[1,2,2,320]{3,2,1,0:T(2,128)} %param.42) | copy-start | bytes 15364
  23.7 18.2 %copy-start.20 = (bf16[9,320,4]{1,2,0:T(4,128)(2,1)S(1)}, bf16[9,320,4]{1,2,0:T(4,128)(2,1)}, u32[]{:S(2)}) copy-start(bf16[9,320,4]{1,2,0:T(4,128)(2,1)} %param.44) | copy-start | bytes 69124
  24.8 9.2 %collective-permute-start = (bf16[2,4,4,128]{3,1,2,0:T(4,128)(2,1)S(1)}, bf16[2,4,4,128]{3,1,2,0:T(4,128)(2,1)S(1)}, u32[]{:S(2)}, u32[]{:S(2)}) collective-permute-start(bf16[2,4,4,128]{3,1,2,0:T(4,128)(2,1)S(1)} %get-tuple-element.322), channel_id=1, source_target_pairs={{112,0},{113,1},{114,2},{115,3},{116,4},{117,5},{118,6},{119,7},{1... | collective-permute-start | bytes 24584 | tf_op jit(solution)/shard_map/ppermute | solution.py:350
  26.1 18.8 %collective-permute-start.3 = (bf16[2,4,320,128]{3,2,1,0:T(8,128)(2,1)S(1)}, bf16[2,4,320,128]{3,2,1,0:T(8,128)(2,1)S(1)}, u32[]{:S(2)}, u32[]{:S(2)}) collective-permute-start(bf16[2,4,320,128]{3,2,1,0:T(8,128)(2,1)S(1)} %get-tuple-element.303), channel_id=1, source_target_pairs={{0,16},{16,32},{32,48},{48,64},{64,80},{80,96},{96,112},{1,17},{17... | collective-permute-start | bytes 1966088 | tf_op jit(solution)/shard_map/ppermute | solution.py:35
  34.0 7.7 %collective-permute-start.1 = (bf16[2,1,4,128]{3,2,1,0:T(4,128)(2,1)S(1)}, bf16[2,1,4,128]{3,2,1,0:T(4,128)(2,1)S(1)}, u32[]{:S(2)}, u32[]{:S(2)}) collective-permute-start(bf16[2,1,4,128]{3,2,1,0:T(4,128)(2,1)S(1)} %get-tuple-element.316), channel_id=1, source_target_pairs={{0,1},{1,2},{2,3},{3,4},{4,5},{5,6},{6,7},{7,8},{8,9},{9,10},{10,1... | collective-permute-start | bytes 6152 | tf_op jit(solution)/shard_map/ppermute | solution.py:24
  35.9 5.8 %collective-permute-start.2 = (bf16[2,1,4,128]{3,2,1,0:T(4,128)(2,1)S(1)}, bf16[2,1,4,128]{3,2,1,0:T(4,128)(2,1)S(1)}, u32[]{:S(2)}, u32[]{:S(2)}) collective-permute-start(bf16[2,1,4,128]{3,2,1,0:T(4,128)(2,1)S(1)} %get-tuple-element.317), channel_id=1, source_target_pairs={{1,0},{2,1},{3,2},{4,3},{5,4},{6,5},{7,6},{8,7},{9,8},{10,9},{11,1... | collective-permute-start | bytes 6152 | tf_op jit(solution)/shard_map/ppermute | solution.py:27
  60.6 4.8 %copy-start.14 = (bf16[2,320,128]{2,1,0:T(8,128)(2,1)S(1)}, bf16[2,320,128]{2,1,0:T(8,128)(2,1)}, u32[]{:S(2)}) copy-start(bf16[2,320,128]{2,1,0:T(8,128)(2,1)} %get-tuple-element.196) | copy-start | bytes 491524
  79.4 4.0 %copy-start.1 = (f32[2,4,320,128]{3,2,1,0:T(8,128)S(1)}, f32[2,4,320,128]{3,2,1,0:T(8,128)}, u32[]{:S(2)}) copy-start(f32[2,4,320,128]{3,2,1,0:T(8,128)} %conv3x3_rows.12) | copy-start | bytes 3932164
  115.6 1.6 copy-start.29
  115.6 1.6 copy-start.31
  125.1 13.2 %copy-start.33 = (f32[320]{0:T(512)S(1)}, f32[320]{0:T(512)}, u32[]{:S(2)}) copy-start(f32[320]{0:T(512)} %param.47) | copy-start | bytes 3844
  125.1 13.2 %copy-start.35 = (f32[320]{0:T(512)S(1)}, f32[320]{0:T(512)}, u32[]{:S(2)}) copy-start(f32[320]{0:T(512)} %param.46) | copy-start | bytes 3844
  136.5 1.7 copy-start.18
  136.5 1.7 copy-start.17
  141.0 1.1 copy-start.36
  141.0 1.1 copy-start.37
  142.3 68.3 %collective-permute-start.4 = (bf16[2,4,4,128]{3,1,2,0:T(4,128)(2,1)S(1)}, bf16[2,4,4,128]{3,1,2,0:T(4,128)(2,1)S(1)}, u32[]{:S(2)}, u32[]{:S(2)}) collective-permute-start(bf16[2,4,4,128]{3,1,2,0:T(4,128)(2,1)S(1)} %get-tuple-element.326), channel_id=1, source_target_pairs={{112,0},{113,1},{114,2},{115,3},{116,4},{117,5},{118,6},{119,7},{1... | collective-permute-start | bytes 24584 | tf_op jit(solution)/shard_map/ppermute | solution.py:350
  210.6 7.8 %collective-permute-start.5 = (bf16[2,1,4,128]{3,2,1,0:T(4,128)(2,1)S(1)}, bf16[2,1,4,128]{3,2,1,0:T(4,128)(2,1)S(1)}, u32[]{:S(2)}, u32[]{:S(2)}) collective-permute-start(bf16[2,1,4,128]{3,2,1,0:T(4,128)(2,1)S(1)} %get-tuple-element.314), channel_id=1, source_target_pairs={{0,1},{1,2},{2,3},{3,4},{4,5},{5,6},{6,7},{7,8},{8,9},{9,10},{10,1... | collective-permute-start | bytes 6152 | tf_op jit(solution)/shard_map/ppermute | solution.py:24
  212.5 5.9 %collective-permute-start.6 = (bf16[2,1,4,128]{3,2,1,0:T(4,128)(2,1)S(1)}, bf16[2,1,4,128]{3,2,1,0:T(4,128)(2,1)S(1)}, u32[]{:S(2)}, u32[]{:S(2)}) collective-permute-start(bf16[2,1,4,128]{3,2,1,0:T(4,128)(2,1)S(1)} %get-tuple-element.315), channel_id=1, source_target_pairs={{1,0},{2,1},{3,2},{4,3},{5,4},{6,5},{7,6},{8,7},{9,8},{10,9},{11,1... | collective-permute-start | bytes 6152 | tf_op jit(solution)/shard_map/ppermute | solution.py:27
  217.1 13.6 %collective-permute-start.7 = (bf16[2,4,320,128]{3,2,1,0:T(8,128)(2,1)S(1)}, bf16[2,4,320,128]{3,2,1,0:T(8,128)(2,1)S(1)}, u32[]{:S(2)}, u32[]{:S(2)}) collective-permute-start(bf16[2,4,320,128]{3,2,1,0:T(8,128)(2,1)S(1)} %get-tuple-element.334), channel_id=1, source_target_pairs={{0,16},{16,32},{32,48},{48,64},{64,80},{80,96},{96,112},{1,17},{17... | collective-permute-start | bytes 1966088 | tf_op jit(solution)/shard_map/ppermute | solution.py:35
  244.8 2.9 copy-start.16
  245.9 1.9 copy-start.15
  247.7 1.3 copy-start.5
  262.2 4.0 %copy-start = (f32[2,4,320,128]{3,2,1,0:T(8,128)S(1)}, f32[2,4,320,128]{3,2,1,0:T(8,128)}, u32[]{:S(2)}) copy-start(f32[2,4,320,128]{3,2,1,0:T(8,128)} %conv3x3_rows.14) | copy-start | bytes 3932164
  (9 other events, 7.4 us)
where the time goes:
time: 387 us; the launch traced here: 380 us
  Pallas kernels  180 us (47%)
  waiting for transfers between devices  81 us (21%)
  other arithmetic  40.3 us (10%)
  local copies, waits for them, and re-layouts  34.8 us (9%)
  starting transfers between devices  19.7 us (5%)
  matrix products  12.6 us (3%)
  loops' own time  7.91 us (2%)
    pallas_call x1, Pallas kernels, scatter_from_last(): pl.pallas_call(lambda *refs: scatter_kernel(count, *refs), out_shape=jax....  73.6 us
    pallas_call x6, Pallas kernels, exchange_patch(): pl.pallas_call(lambda *refs: exchange_kernel(peers, *refs), out_shape=(ja...  73.1 us
    ppermute x2, waiting for transfers between devices, per_device(): scaled_first = lax.ppermute(scaled, 'segment', [(last, 0)])  71.9 us
    pallas_call x4, Pallas kernels, conv_wide(): pl.pallas_call(conv_kernel, grid=(1,), out_shape=jax.ShapeDtypeStruct(out...  33.4 us
    convert_element_type x10, other arithmetic, act_with_rows(): return jnp.where(pad, 0.0, act).astype(jnp.bfloat16)  14.5 us
    dot_general x36, matrix products, conv_valid(): jnp.einsum('oi,bhiw->bhow', kernel[tap_no], window, preferred_element_typ...  12.6 us
    ppermute x2, waiting for transfers between devices, from_behind(): return lax.ppermute(shard, axis, pairs)  9.11 us
    ppermute x2, starting transfers between devices, with_halo(): lax.ppermute(lax.slice_in_dim(block, 0, width, axis=dim), axis, backward)  9.08 us
  transfers between devices with their start and end apart: 8, of which 3 were waited for; matrix products, arithmetic and copies ran while one was open for 2% of the time, Pallas kernels for 0%

commit v1 on v0

--- a/solution.py
+++ b/solution.py
@@ -48,17 +48,41 @@
 
 
 def exchange_kernel(
-    peers, x_ref, top_ref, bot_ref, o_ref, lo_ref, hi_ref, send_sem, recv_sem, row_send, row_recv
+    peers, x_ref, top_ref, bot_ref, o_ref, lo_ref, hi_ref, quad_sem, cross_sem, own_sem, row_send, row_recv
 ):
     me = lax.axis_index("patch")
     seg = lax.axis_index("segment")
     mesh_ids = pl.DeviceIdType.MESH
+    quad = 4
+    groups = peers // quad
+    pos = me % quad
+    group = me // quad
+    first_in_group = (pos == 0) & (group > 0)
+    last_in_group = (pos == quad - 1) & (group < groups - 1)
+    quad_peers = [group * quad + (pos + d) % quad for d in range(1, quad)]
+    cross_peers = [((group + d) % groups) * quad + pos for d in range(1, groups)]
     barrier = pltpu.get_barrier_semaphore()
-    for dist in range(1, peers):
-        pl.semaphore_signal(
-            barrier, 1, device_id=(seg, lax.rem(me + dist, peers)), device_id_type=mesh_ids
-        )
-    pl.semaphore_wait(barrier, peers - 1)
+    for peer in quad_peers + cross_peers:
+        pl.semaphore_signal(barrier, 1, device_id=(seg, peer), device_id_type=mesh_ids)
+
+    @pl.when(first_in_group)
+    def _():
+        pl.semaphore_signal(barrier, 1, device_id=(seg, me - 1), device_id_type=mesh_ids)
+
+    @pl.when(last_in_group)
+    def _():
+        pl.semaphore_signal(barrier, 1, device_id=(seg, me + 1), device_id_type=mesh_ids)
+
+    greeted = len(quad_peers) + len(cross_peers)
+
+    @pl.when(first_in_group | last_in_group)
+    def _():
+        pl.semaphore_wait(barrier, greeted + 1)
+
+    @pl.when(jnp.logical_not(first_in_group | last_in_group))
+    def _():
+        pl.semaphore_wait(barrier, greeted)
+
     down = pltpu.make_async_remote_copy(
         src_ref=bot_ref,
         dst_ref=lo_ref,
@@ -84,19 +108,20 @@
     def _():
         up.start()
 
-    copies = []
-    for dist in range(1, peers):
+    own = pltpu.make_async_copy(x_ref, o_ref.at[me], own_sem.at[0])
+    own.start()
+    near = []
+    for d, peer in enumerate(quad_peers):
         copy = pltpu.make_async_remote_copy(
             src_ref=x_ref,
             dst_ref=o_ref.at[me],
-            send_sem=send_sem.at[dist],
-            recv_sem=recv_sem.at[dist],
-            device_id=(seg, lax.rem(me + dist, peers)),
+            send_sem=quad_sem.at[0, d],
+            recv_sem=quad_sem.at[1, d],
+            device_id=(seg, peer),
             device_id_type=mesh_ids,
         )
         copy.start()
-        copies.append(copy)
-    o_ref[me] = x_ref[...]
+        near.append(copy)
 
     @pl.when(me == 0)
     def _():
@@ -106,7 +131,23 @@
     def _():
         hi_ref[...] = jnp.zeros(hi_ref.shape, hi_ref.dtype)
 
-    for copy in copies:
+    own.wait()
+    for copy in near:
+        copy.wait()
+    block = o_ref.at[pl.ds(group * quad, quad)]
+    far = []
+    for d, peer in enumerate(cross_peers):
+        copy = pltpu.make_async_remote_copy(
+            src_ref=block,
+            dst_ref=block,
+            send_sem=cross_sem.at[0, d],
+            recv_sem=cross_sem.at[1, d],
+            device_id=(seg, peer),
+            device_id_type=mesh_ids,
+        )
+        copy.start()
+        far.append(copy)
+    for copy in far:
         copy.wait()
 
     @pl.when(me < peers - 1)
@@ -133,8 +174,9 @@
         in_specs=[vmem] * 3,
         out_specs=(vmem, vmem, vmem),
         scratch_shapes=[
-            pltpu.SemaphoreType.DMA((peers,)),
-            pltpu.SemaphoreType.DMA((peers,)),
+            pltpu.SemaphoreType.DMA((2, 3)),
+            pltpu.SemaphoreType.DMA((2, peers // 4 - 1)),
+            pltpu.SemaphoreType.DMA((1,)),
             pltpu.SemaphoreType.DMA((2,)),
             pltpu.SemaphoreType.DMA((2,)),
         ],

time: 387 us -> 408 us (1.054)
  the two profiles are of different devices: /device:TPU:2 before, /device:TPU:0 now
where the time goes in v1:
time: 408 us; the launch traced here: 401 us
  Pallas kernels  224 us (55%)
  other arithmetic  71.8 us (18%)
  local copies, waits for them, and re-layouts  50.8 us (12%)
  waiting for transfers between devices  25.7 us (6%)
  matrix products  12.6 us (3%)
  starting transfers between devices  11.9 us (3%)
    pallas_call x10, Pallas kernels, exchange_patch(): pl.pallas_call(lambda *refs: exchange_kernel(peers, *refs), out_shape=(ja...  149 us
    pallas_call x8, Pallas kernels, conv_wide(): pl.pallas_call(conv_kernel, grid=(1,), out_shape=jax.ShapeDtypeStruct(out...  66.7 us
    convert_element_type x18, other arithmetic, act_with_rows(): return jnp.where(pad, 0.0, act).astype(jnp.bfloat16)  26.1 us
    another operation x8, other arithmetic, conv_wide(): shifted = jnp.stack([padded[..., j:j + cols] for j in range(3)])  15.3 us
    ppermute x2, waiting for transfers between devices, per_device(): scaled_first = lax.ppermute(scaled, 'segment', [(last, 0)])  12.8 us
    dot_general x36, matrix products, conv_valid(): jnp.einsum('oi,bhiw->bhow', kernel[tap_no], window, preferred_element_typ...  12.6 us
    ppermute x2, waiting for transfers between devices, from_behind(): return lax.ppermute(shard, axis, pairs)  11.2 us
    squeeze x10, local copies, waits for them, and re-layouts, group_moments(): every, low, high = exchange_patch(packed, rows[:, 0], rows[:, height - 1])  9.99 us
  transfers between devices with their start and end apart: 8, of which 5 were waited for; matrix products, arithmetic and copies ran while one was open for 2% of the time, Pallas kernels for 0%

profile of v1, /device:TPU:0, one launch (start us, length us, event | category | flops | bytes accessed | tf_op | source)
XLA Modules:
  0.0 400.6 jit_solution(9332498498839946024)
XLA Ops:
  5.9 14.9 %exchange_stats_rows.14 = (f32[16,8,128]{2,1,0:T(8,128)}, bf16[2,320,128]{2,1,0:T(8,128)(2,1)}, bf16[2,320,128]{2,1,0:T(8,128)(2,1)}) custom-call(f32[8,128]{1,0:T(8,128)} %scatter.36.refs_0_, bf16[2,320,128]{2,1,0:T(8,128)(2,1)} %get-tuple-element.305.refs_1_, bf16[2,320,128]{2,1,0:T(8,128)(2,1)} %get-tuple-element.304.refs_2_), custom_call_target="tpu_custom_call" | custom-call | tf_op jit(solution)/shard_map/exchange_stats_rows/pallas_call | solution.py:167
  29.3 2.9 collective-permute-start.3
  32.2 5.0 %collective-permute-done = bf16[2,4,4,128]{3,1,2,0:T(4,128)(2,1)S(1)} collective-permute-done((bf16[2,4,4,128]{3,1,2,0:T(4,128)(2,1)S(1)}, bf16[2,4,4,128]{3,1,2,0:T(4,128)(2,1)S(1)}, u32[]{:S(2)}, u32[]{:S(2)}) %collective-permute-start) | collective-permute-done | bytes 8224 | tf_op jit(solution)/shard_map/ppermute | solution.py:392
  48.7 16.3 %exchange_stats_rows.15 = (f32[16,8,128]{2,1,0:T(8,128)}, bf16[2,320,128]{2,1,0:T(8,128)(2,1)}, bf16[2,320,128]{2,1,0:T(8,128)(2,1)}) custom-call(f32[8,128]{1,0:T(8,128)} %scatter.37.refs_0_, bf16[2,320,128]{2,1,0:T(8,128)(2,1)} %get-tuple-element.301.refs_1_, bf16[2,320,128]{2,1,0:T(8,128)(2,1)} %get-tuple-element.300.refs_2_), custom_call_target="tpu_custom_call" | custom-call | tf_op jit(solution)/shard_map/exchange_stats_rows/pallas_call | solution.py:167
  75.3 1.9 pad_maximum_fusion.4.x_ref
  77.2 8.3 %conv3x3_rows.12 = f32[2,4,320,128]{3,2,1,0:T(8,128)} custom-call(bf16[3,2,6,320,128]{4,3,2,1,0:T(8,128)(2,1)} %pad_maximum_fusion.4.x_ref, bf16[1,2,9,320,320]{4,3,2,1,0:T(8,128)(2,1)} %w_ref.6), custom_call_target="tpu_custom_call" | custom-call | flops 1887436800 | bytes 6103040 | tf_op jit(solution)/shard_map/conv3x3_rows/pallas_call | solution.py:314
  87.4 1.9 slice_bitcast_fusion.12
  90.9 15.7 %exchange_stats_rows.16 = (f32[16,8,128]{2,1,0:T(8,128)}, f32[2,320,128]{2,1,0:T(8,128)}, f32[2,320,128]{2,1,0:T(8,128)}) custom-call(f32[8,128]{1,0:T(8,128)} %scatter.38.refs_0_, f32[2,320,128]{2,1,0:T(8,128)} %get-tuple-element.283.refs_1_, f32[2,320,128]{2,1,0:T(8,128)} %get-tuple-element.282.refs_2_), custom_call_target="tpu_custom_call" | custom-call | tf_op jit(solution)/shard_map/exchange_stats_rows/pallas_call | solution.py:167
  108.1 2.1 select_convert_fusion.14
  114.4 8.3 %conv3x3_rows.13 = f32[2,4,320,128]{3,2,1,0:T(8,128)} custom-call(bf16[3,2,6,320,128]{4,3,2,1,0:T(8,128)(2,1)} %pad_maximum_fusion.5.x_ref, bf16[1,2,9,320,320]{4,3,2,1,0:T(8,128)(2,1)} %w_ref.7), custom_call_target="tpu_custom_call" | custom-call | flops 1887436800 | bytes 6103040 | tf_op jit(solution)/shard_map/conv3x3_rows/pallas_call | solution.py:314
  124.4 70.6 %conditional.2 = (bf16[2,4,320,128]{3,2,1,0:T(8,128)(2,1)S(1)}) conditional(s32[]{:T(128)} %bitcast.85, bf16[2,4,320,128]{3,2,1,0:T(8,128)(2,1)S(1)} %add_convert_fusion.3, (bf16[2,4,320,128]{3,2,1,0:T(8,128)(2,1)S(1)}, f32[1,2,2,320]{3,2,1,0:T(2,128)S(1)}, f32[1,2,2,320]{3,2,1,0:T(2,128)S(1)}, bf16[1,2,9,320,320]{4,3,2,1,0:T(8,128)(2,1)}, ...), branch_computations={%region_21.22_spmd, %region_22.37_spmd} | conditional | flops 3809128960 | bytes 63341760 | solution.py:398
  127.2 13.3 %exchange_stats_rows.10 = (f32[16,8,128]{2,1,0:T(8,128)}, bf16[2,320,128]{2,1,0:T(8,128)(2,1)}, bf16[2,320,128]{2,1,0:T(8,128)(2,1)}) custom-call(f32[8,128]{1,0:T(8,128)} %scatter.10.refs_0_, bf16[2,320,128]{2,1,0:T(8,128)(2,1)} %get-tuple-element.253.refs_1_, bf16[2,320,128]{2,1,0:T(8,128)(2,1)} %get-tuple-element.252.refs_2_), custom_call_target="tpu_custom_call" | custom-call | tf_op jit(solution)/shard_map/cond/branch_1_fun/exchange_stats_rows/pallas_call | solution.py:167
  148.4 8.3 %conv3x3_rows.8 = f32[2,4,320,128]{3,2,1,0:T(8,128)} custom-call(bf16[3,2,6,320,128]{4,3,2,1,0:T(8,128)(2,1)} %pad_maximum_fusion.x_ref, bf16[1,2,9,320,320]{4,3,2,1,0:T(8,128)(2,1)} %get-tuple-element.154.w_ref), custom_call_target="tpu_custom_call" | custom-call | flops 1887436800 | bytes 6103040 | tf_op jit(solution)/shard_map/cond/branch_1_fun/conv3x3_rows/pallas_call | solution.py:314
  160.9 16.5 %exchange_stats_rows.11 = (f32[16,8,128]{2,1,0:T(8,128)}, f32[2,320,128]{2,1,0:T(8,128)}, f32[2,320,128]{2,1,0:T(8,128)}) custom-call(f32[8,128]{1,0:T(8,128)} %scatter.11.refs_0_, f32[2,320,128]{2,1,0:T(8,128)} %get-tuple-element.245.refs_1_, f32[2,320,128]{2,1,0:T(8,128)} %get-tuple-element.244.refs_2_), custom_call_target="tpu_custom_call" | custom-call | tf_op jit(solution)/shard_map/cond/branch_1_fun/exchange_stats_rows/pallas_call | solution.py:167
  179.0 2.1 select_convert_fusion
  184.9 8.3 %conv3x3_rows.9 = f32[2,4,320,128]{3,2,1,0:T(8,128)} custom-call(bf16[3,2,6,320,128]{4,3,2,1,0:T(8,128)(2,1)} %pad_maximum_fusion.1.x_ref, bf16[1,2,9,320,320]{4,3,2,1,0:T(8,128)(2,1)} %get-tuple-element.158.w_ref), custom_call_target="tpu_custom_call" | custom-call | flops 1887436800 | bytes 6103040 | tf_op jit(solution)/shard_map/cond/branch_1_fun/conv3x3_rows/pallas_call | solution.py:314
  197.8 12.5 %exchange_stats_rows.17 = (f32[16,8,128]{2,1,0:T(8,128)}, bf16[2,320,128]{2,1,0:T(8,128)(2,1)}, bf16[2,320,128]{2,1,0:T(8,128)(2,1)}) custom-call(f32[8,128]{1,0:T(8,128)} %scatter.41.refs_0_, bf16[2,320,128]{2,1,0:T(8,128)(2,1)} %get-tuple-element.297.refs_1_, bf16[2,320,128]{2,1,0:T(8,128)(2,1)} %get-tuple-element.296.refs_2_), custom_call_target="tpu_custom_call" | custom-call | tf_op jit(solution)/shard_map/exchange_stats_rows/pallas_call | solution.py:167
  217.4 7.9 %collective-permute-done.4 = bf16[2,4,4,128]{3,1,2,0:T(4,128)(2,1)S(1)} collective-permute-done((bf16[2,4,4,128]{3,1,2,0:T(4,128)(2,1)S(1)}, bf16[2,4,4,128]{3,1,2,0:T(4,128)(2,1)S(1)}, u32[]{:S(2)}, u32[]{:S(2)}) %collective-permute-start.4) | collective-permute-done | bytes 8224 | tf_op jit(solution)/shard_map/ppermute | solution.py:392
  232.7 11.2 %collective-permute-done.7 = bf16[2,4,320,128]{3,2,1,0:T(8,128)(2,1)S(1)} collective-permute-done((bf16[2,4,320,128]{3,2,1,0:T(8,128)(2,1)S(1)}, bf16[2,4,320,128]{3,2,1,0:T(8,128)(2,1)S(1)}, u32[]{:S(2)}, u32[]{:S(2)}) %collective-permute-start.7) | collective-permute-done | bytes 655392 | tf_op jit(solution)/shard_map/ppermute | solution.py:35
  247.0 14.6 %exchange_stats_rows.18 = (f32[16,8,128]{2,1,0:T(8,128)}, bf16[2,320,128]{2,1,0:T(8,128)(2,1)}, bf16[2,320,128]{2,1,0:T(8,128)(2,1)}) custom-call(f32[8,128]{1,0:T(8,128)} %scatter.42.refs_0_, bf16[2,320,128]{2,1,0:T(8,128)(2,1)} %get-tuple-element.295.refs_1_, bf16[2,320,128]{2,1,0:T(8,128)(2,1)} %get-tuple-element.294.refs_2_), custom_call_target="tpu_custom_call" | custom-call | tf_op jit(solution)/shard_map/exchange_stats_rows/pallas_call | solution.py:167
  270.8 8.3 %conv3x3_rows.14 = f32[2,4,320,128]{3,2,1,0:T(8,128)} custom-call(bf16[3,2,6,320,128]{4,3,2,1,0:T(8,128)(2,1)} %pad_maximum_fusion.6.x_ref, bf16[1,2,9,320,320]{4,3,2,1,0:T(8,128)(2,1)} %w_ref.6), custom_call_target="tpu_custom_call" | custom-call | flops 1887436800 | bytes 6103040 | tf_op jit(solution)/shard_map/conv3x3_rows/pallas_call | solution.py:314
  281.0 1.9 slice_bitcast_fusion.10
  284.4 16.2 %exchange_stats_rows.19 = (f32[16,8,128]{2,1,0:T(8,128)}, f32[2,320,128]{2,1,0:T(8,128)}, f32[2,320,128]{2,1,0:T(8,128)}) custom-call(f32[8,128]{1,0:T(8,128)} %scatter.43.refs_0_, f32[2,320,128]{2,1,0:T(8,128)} %get-tuple-element.281.refs_1_, f32[2,320,128]{2,1,0:T(8,128)} %get-tuple-element.280.refs_2_), custom_call_target="tpu_custom_call" | custom-call | tf_op jit(solution)/shard_map/exchange_stats_rows/pallas_call | solution.py:167
  302.1 2.1 select_convert_fusion.9
  308.5 8.3 %conv3x3_rows.15 = f32[2,4,320,128]{3,2,1,0:T(8,128)} custom-call(bf16[3,2,6,320,128]{4,3,2,1,0:T(8,128)(2,1)} %pad_maximum_fusion.7.x_ref, bf16[1,2,9,320,320]{4,3,2,1,0:T(8,128)(2,1)} %w_ref.7), custom_call_target="tpu_custom_call" | custom-call | flops 1887436800 | bytes 6103040 | tf_op jit(solution)/shard_map/conv3x3_rows/pallas_call | solution.py:314
  318.4 69.7 %conditional.3 = (bf16[2,4,320,128]{3,2,1,0:T(8,128)(2,1)S(1)}) conditional(s32[]{:T(128)} %bitcast.85, bf16[2,4,320,128]{3,2,1,0:T(8,128)(2,1)S(1)} %add_convert_fusion.2, (bf16[2,4,320,128]{3,2,1,0:T(8,128)(2,1)S(1)}, f32[1,2,2,320]{3,2,1,0:T(2,128)S(1)}, f32[1,2,2,320]{3,2,1,0:T(2,128)S(1)}, bf16[1,2,9,320,320]{4,3,2,1,0:T(8,128)(2,1)}, ...), branch_computations={%region_58.59_spmd, %region_59.74_spmd} | conditional | flops 3809128960 | bytes 63341760 | solution.py:398
  321.2 12.8 %exchange_stats_rows.12 = (f32[16,8,128]{2,1,0:T(8,128)}, bf16[2,320,128]{2,1,0:T(8,128)(2,1)}, bf16[2,320,128]{2,1,0:T(8,128)(2,1)}) custom-call(f32[8,128]{1,0:T(8,128)} %scatter.20.refs_0_, bf16[2,320,128]{2,1,0:T(8,128)(2,1)} %get-tuple-element.271.refs_1_, bf16[2,320,128]{2,1,0:T(8,128)(2,1)} %get-tuple-element.270.refs_2_), custom_call_target="tpu_custom_call" | custom-call | tf_op jit(solution)/shard_map/cond/branch_1_fun/exchange_stats_rows/pallas_call | solution.py:167
  341.8 8.3 %conv3x3_rows.10 = f32[2,4,320,128]{3,2,1,0:T(8,128)} custom-call(bf16[3,2,6,320,128]{4,3,2,1,0:T(8,128)(2,1)} %pad_maximum_fusion.2.x_ref, bf16[1,2,9,320,320]{4,3,2,1,0:T(8,128)(2,1)} %get-tuple-element.165.w_ref), custom_call_target="tpu_custom_call" | custom-call | flops 1887436800 | bytes 6103040 | tf_op jit(solution)/shard_map/cond/branch_1_fun/conv3x3_rows/pallas_call | solution.py:314
  354.4 16.0 %exchange_stats_rows.13 = (f32[16,8,128]{2,1,0:T(8,128)}, f32[2,320,128]{2,1,0:T(8,128)}, f32[2,320,128]{2,1,0:T(8,128)}) custom-call(f32[8,128]{1,0:T(8,128)} %scatter.21.refs_0_, f32[2,320,128]{2,1,0:T(8,128)} %get-tuple-element.263.refs_1_, f32[2,320,128]{2,1,0:T(8,128)} %get-tuple-element.262.refs_2_), custom_call_target="tpu_custom_call" | custom-call | tf_op jit(solution)/shard_map/cond/branch_1_fun/exchange_stats_rows/pallas_call | solution.py:167
  372.0 2.1 select_convert_fusion.4
  377.9 8.3 %conv3x3_rows.11 = f32[2,4,320,128]{3,2,1,0:T(8,128)} custom-call(bf16[3,2,6,320,128]{4,3,2,1,0:T(8,128)(2,1)} %pad_maximum_fusion.3.x_ref, bf16[1,2,9,320,320]{4,3,2,1,0:T(8,128)(2,1)} %get-tuple-element.169.w_ref), custom_call_target="tpu_custom_call" | custom-call | flops 1887436800 | bytes 6103040 | tf_op jit(solution)/shard_map/cond/branch_1_fun/conv3x3_rows/pallas_call | solution.py:314
  389.0 8.6 %scatter_latent_columns.1 = f32[4,128]{1,0:T(4,128)} custom-call(f32[8,4,128]{2,1,0:T(4,128)} %reshape.1690.refs_0_), custom_call_target="tpu_custom_call" | custom-call | tf_op jit(solution)/shard_map/scatter_latent_columns/pallas_call | solution.py:272
  (443 shorter events, 131.7 us)
Async XLA Ops:
  0.6 3.2 copy-start.4
  3.6 19.8 %copy-start.32 = (f32[320]{0:T(512)S(1)}, f32[320]{0:T(512)}, u32[]{:S(2)}) copy-start(f32[320]{0:T(512)} %param.47) | copy-start | bytes 3844
  3.6 19.8 %copy-start.34 = (f32[320]{0:T(512)S(1)}, f32[320]{0:T(512)}, u32[]{:S(2)}) copy-start(f32[320]{0:T(512)} %param.46) | copy-start | bytes 3844
  22.3 2.3 copy-start.23
  22.3 2.3 copy-start.19
  26.1 1.7 copy-start.27
  26.9 12.9 %copy-start.28 = (f32[1,2,2,320]{3,2,1,0:T(2,128)S(1)}, f32[1,2,2,320]{3,2,1,0:T(2,128)}, u32[]{:S(2)}) copy-start(f32[1,2,2,320]{3,2,1,0:T(2,128)} %param.43) | copy-start | bytes 15364
  26.9 12.9 %copy-start.30 = (f32[1,2,2,320]{3,2,1,0:T(2,128)S(1)}, f32[1,2,2,320]{3,2,1,0:T(2,128)}, u32[]{:S(2)}) copy-start(f32[1,2,2,320]{3,2,1,0:T(2,128)} %param.42) | copy-start | bytes 15364
  26.9 15.6 %copy-start.20 = (bf16[9,320,4]{1,2,0:T(4,128)(2,1)S(1)}, bf16[9,320,4]{1,2,0:T(4,128)(2,1)}, u32[]{:S(2)}) copy-start(bf16[9,320,4]{1,2,0:T(4,128)(2,1)} %param.44) | copy-start | bytes 69124
  28.0 9.2 %collective-permute-start = (bf16[2,4,4,128]{3,1,2,0:T(4,128)(2,1)S(1)}, bf16[2,4,4,128]{3,1,2,0:T(4,128)(2,1)S(1)}, u32[]{:S(2)}, u32[]{:S(2)}) collective-permute-start(bf16[2,4,4,128]{3,1,2,0:T(4,128)(2,1)S(1)} %get-tuple-element.322), channel_id=1, source_target_pairs={{112,0},{113,1},{114,2},{115,3},{116,4},{117,5},{118,6},{119,7},{1... | collective-permute-start | bytes 24584 | tf_op jit(solution)/shard_map/ppermute | solution.py:392
  29.3 16.2 %collective-permute-start.3 = (bf16[2,4,320,128]{3,2,1,0:T(8,128)(2,1)S(1)}, bf16[2,4,320,128]{3,2,1,0:T(8,128)(2,1)S(1)}, u32[]{:S(2)}, u32[]{:S(2)}) collective-permute-start(bf16[2,4,320,128]{3,2,1,0:T(8,128)(2,1)S(1)} %get-tuple-element.303), channel_id=1, source_target_pairs={{0,16},{16,32},{32,48},{48,64},{64,80},{80,96},{96,112},{1,17},{17... | collective-permute-start | bytes 1966088 | tf_op jit(solution)/shard_map/ppermute | solution.py:35
  37.2 3.9 collective-permute-start.1
  38.5 3.9 collective-permute-start.2
  66.7 4.8 %copy-start.14 = (bf16[2,320,128]{2,1,0:T(8,128)(2,1)S(1)}, bf16[2,320,128]{2,1,0:T(8,128)(2,1)}, u32[]{:S(2)}) copy-start(bf16[2,320,128]{2,1,0:T(8,128)(2,1)} %get-tuple-element.196) | copy-start | bytes 491524
  85.5 4.0 %copy-start.1 = (f32[2,4,320,128]{3,2,1,0:T(8,128)S(1)}, f32[2,4,320,128]{3,2,1,0:T(8,128)}, u32[]{:S(2)}) copy-start(f32[2,4,320,128]{3,2,1,0:T(8,128)} %conv3x3_rows.12) | copy-start | bytes 3932164
  156.7 2.1 copy-start.2
  177.4 3.8 copy-start.10
  177.4 3.8 copy-start.11
  196.8 15.3 %copy-start.33 = (f32[320]{0:T(512)S(1)}, f32[320]{0:T(512)}, u32[]{:S(2)}) copy-start(f32[320]{0:T(512)} %param.47) | copy-start | bytes 3844
  196.8 15.3 %copy-start.35 = (f32[320]{0:T(512)S(1)}, f32[320]{0:T(512)}, u32[]{:S(2)}) copy-start(f32[320]{0:T(512)} %param.46) | copy-start | bytes 3844
  210.3 1.7 copy-start.18
  210.3 1.7 copy-start.17
  216.1 9.2 %collective-permute-start.4 = (bf16[2,4,4,128]{3,1,2,0:T(4,128)(2,1)S(1)}, bf16[2,4,4,128]{3,1,2,0:T(4,128)(2,1)S(1)}, u32[]{:S(2)}, u32[]{:S(2)}) collective-permute-start(bf16[2,4,4,128]{3,1,2,0:T(4,128)(2,1)S(1)} %get-tuple-element.326), channel_id=1, source_target_pairs={{112,0},{113,1},{114,2},{115,3},{116,4},{117,5},{118,6},{119,7},{1... | collective-permute-start | bytes 24584 | tf_op jit(solution)/shard_map/ppermute | solution.py:392
  225.3 3.9 collective-permute-start.5
  226.5 3.1 collective-permute-start.6
  227.8 16.0 %collective-permute-start.7 = (bf16[2,4,320,128]{3,2,1,0:T(8,128)(2,1)S(1)}, bf16[2,4,320,128]{3,2,1,0:T(8,128)(2,1)S(1)}, u32[]{:S(2)}, u32[]{:S(2)}) collective-permute-start(bf16[2,4,320,128]{3,2,1,0:T(8,128)(2,1)S(1)} %get-tuple-element.334), channel_id=1, source_target_pairs={{0,16},{16,32},{32,48},{48,64},{64,80},{80,96},{96,112},{1,17},{17... | collective-permute-start | bytes 1966088 | tf_op jit(solution)/shard_map/ppermute | solution.py:35
  261.6 2.9 copy-start.16
  262.8 1.9 copy-start.15
  279.1 4.0 %copy-start = (f32[2,4,320,128]{3,2,1,0:T(8,128)S(1)}, f32[2,4,320,128]{3,2,1,0:T(8,128)}, u32[]{:S(2)}) copy-start(f32[2,4,320,128]{3,2,1,0:T(8,128)} %conv3x3_rows.14) | copy-start | bytes 3932164
  350.2 2.1 copy-start.3
  370.4 3.8 copy-start.12
  370.4 3.8 copy-start.13
  (15 other events, 15.7 us)

commit v2 on v0

--- a/solution.py
+++ b/solution.py
@@ -339,7 +339,12 @@
     current = jnp.transpose(features[0], (0, 2, 1, 3))
     for step_no in range(STEPS):
         arrived = from_behind(current, "segment", 1)
-        noise_local = head_noise(current, head_w, head_gain, head_shift)
+        noise_local = lax.cond(
+            segment_pos == last,
+            lambda source: head_noise(source, head_w, head_gain, head_shift),
+            lambda source: jnp.zeros(latent.shape, jnp.float32),
+            current,
+        )
         position = plan_pos + step_no
         sigma_now = sigma_at(position)
         sigma_next = sigma_at(position + 1)

time: 387 us -> 371 us (0.959)
  waiting for transfers between devices: 81 us -> 47.9 us
  other arithmetic: 40.3 us -> 64.2 us
  local copies, waits for them, and re-layouts: 34.8 us -> 43.2 us
  loops' own time: 7.91 us -> 0.98 us
  matrix products: 12.6 us -> 7.12 us
    pallas_call x1, Pallas kernels: 73.6 us -> 10.6 us  [scatter_from_last(): pl.pallas_call(lambda *refs: scatter_kernel(count, *refs), out_shape=jax....]
    ppermute x2, waiting for transfers between devices: 71.9 us -> 38.2 us  [per_device(): scaled_first = lax.ppermute(scaled, 'segment', [(last, 0)])]
    pallas_call x4 -> x8, Pallas kernels: 33.4 us -> 66.7 us  [conv_wide(): pl.pallas_call(conv_kernel, grid=(1,), out_shape=jax.ShapeDtypeStruct(out...]
    pallas_call x6 -> x8, Pallas kernels: 73.1 us -> 101 us  [exchange_patch(): pl.pallas_call(lambda *refs: exchange_kernel(peers, *refs), out_shape=(ja...]
    convert_element_type x10 -> x16, other arithmetic: 14.5 us -> 23 us  [act_with_rows(): return jnp.where(pad, 0.0, act).astype(jnp.bfloat16)]
    another operation x4 -> x8, other arithmetic: 7.66 us -> 15.3 us  [conv_wide(): shifted = jnp.stack([padded[..., j:j + cols] for j in range(3)])]
    another operation x2, loops' own time: 7.91 us -> 0.93 us  [per_device(): lax.cond(blocks_used[0] >= 2, lambda hidden: resnet_unit(hidden, conv1_w,...]
    dot_general x36 -> x18, matrix products: 12.6 us -> 7.12 us  [conv_valid(): jnp.einsum('oi,bhiw->bhow', kernel[tap_no], window, preferred_element_typ...]
  transfers between devices with their start and end apart: 8 -> 8, of which waited for: 3 -> 4; matrix products, arithmetic and copies ran while one was open for 2% -> 2% of each run, Pallas kernels for 0% -> 0%
where the time goes in v2:
time: 371 us; the launch traced here: 364 us
  Pallas kernels  178 us (48%)
  other arithmetic  64.2 us (17%)
  waiting for transfers between devices  47.9 us (13%)
  local copies, waits for them, and re-layouts  43.2 us (12%)
  starting transfers between devices  20.3 us (5%)
  matrix products  7.12 us (2%)
    pallas_call x8, Pallas kernels, exchange_patch(): pl.pallas_call(lambda *refs: exchange_kernel(peers, *refs), out_shape=(ja...  101 us
    pallas_call x8, Pallas kernels, conv_wide(): pl.pallas_call(conv_kernel, grid=(1,), out_shape=jax.ShapeDtypeStruct(out...  66.7 us
    ppermute x2, waiting for transfers between devices, per_device(): scaled_first = lax.ppermute(scaled, 'segment', [(last, 0)])  38.2 us
    convert_element_type x16, other arithmetic, act_with_rows(): return jnp.where(pad, 0.0, act).astype(jnp.bfloat16)  23 us
    another operation x8, other arithmetic, conv_wide(): shifted = jnp.stack([padded[..., j:j + cols] for j in range(3)])  15.3 us
    pallas_call x1, Pallas kernels, scatter_from_last(): pl.pallas_call(lambda *refs: scatter_kernel(count, *refs), out_shape=jax....  10.6 us
    ppermute x2, waiting for transfers between devices, from_behind(): return lax.ppermute(shard, axis, pairs)  9.09 us
    ppermute x2, starting transfers between devices, with_halo(): lax.ppermute(lax.slice_in_dim(block, 0, width, axis=dim), axis, backward)  9.08 us
  transfers between devices with their start and end apart: 8, of which 4 were waited for; matrix products, arithmetic and copies ran while one was open for 2% of the time, Pallas kernels for 0%

profile of v2, /device:TPU:2, one launch (start us, length us, event | category | flops | bytes accessed | tf_op | source)
XLA Modules:
  0.0 364.0 jit_solution(7358148219720172767)
XLA Ops:
  0.6 2.0 copy.141
  2.6 3.5 collective-permute-start.3
  9.6 30.3 %collective-permute-done = bf16[2,4,4,128]{3,1,2,0:T(4,128)(2,1)S(1)} collective-permute-done((bf16[2,4,4,128]{3,1,2,0:T(4,128)(2,1)S(1)}, bf16[2,4,4,128]{3,1,2,0:T(4,128)(2,1)S(1)}, u32[]{:S(2)}, u32[]{:S(2)}) %collective-permute-start) | collective-permute-done | bytes 8224 | tf_op jit(solution)/shard_map/ppermute | solution.py:355
  41.8 4.5 %collective-permute-start.2 = (bf16[2,1,4,128]{3,2,1,0:T(4,128)(2,1)S(1)}, bf16[2,1,4,128]{3,2,1,0:T(4,128)(2,1)S(1)}, u32[]{:S(2)}, u32[]{:S(2)}) collective-permute-start(bf16[2,1,4,128]{3,2,1,0:T(4,128)(2,1)S(1)} %get-tuple-element.361), channel_id=1, source_target_pairs={{1,0},{2,1},{3,2},{4,3},{5,4},{6,5},{7,6},{8,7},{9,8},{10,9},{11,1... | collective-permute-start | bytes 6152 | tf_op jit(solution)/shard_map/ppermute | solution.py:27
  53.9 10.9 %exchange_stats_rows.16 = (f32[16,8,128]{2,1,0:T(8,128)}, bf16[2,320,128]{2,1,0:T(8,128)(2,1)}, bf16[2,320,128]{2,1,0:T(8,128)(2,1)}) custom-call(f32[8,128]{1,0:T(8,128)} %scatter.38.refs_0_, bf16[2,320,128]{2,1,0:T(8,128)(2,1)} %get-tuple-element.349.refs_1_, bf16[2,320,128]{2,1,0:T(8,128)(2,1)} %get-tuple-element.348.refs_2_), custom_call_target="tpu_custom_call" | custom-call | tf_op jit(solution)/shard_map/exchange_stats_rows/pallas_call | solution.py:126
  72.6 8.3 %conv3x3_rows.12 = f32[2,4,320,128]{3,2,1,0:T(8,128)} custom-call(bf16[3,2,6,320,128]{4,3,2,1,0:T(8,128)(2,1)} %pad_maximum_fusion.4.x_ref, bf16[1,2,9,320,320]{4,3,2,1,0:T(8,128)(2,1)} %w_ref.6), custom_call_target="tpu_custom_call" | custom-call | flops 1887436800 | bytes 6103040 | tf_op jit(solution)/shard_map/conv3x3_rows/pallas_call | solution.py:272
  82.8 1.9 slice_bitcast_fusion.16
  86.3 14.7 %exchange_stats_rows.17 = (f32[16,8,128]{2,1,0:T(8,128)}, f32[2,320,128]{2,1,0:T(8,128)}, f32[2,320,128]{2,1,0:T(8,128)}) custom-call(f32[8,128]{1,0:T(8,128)} %scatter.39.refs_0_, f32[2,320,128]{2,1,0:T(8,128)} %get-tuple-element.333.refs_1_, f32[2,320,128]{2,1,0:T(8,128)} %get-tuple-element.332.refs_2_), custom_call_target="tpu_custom_call" | custom-call | tf_op jit(solution)/shard_map/exchange_stats_rows/pallas_call | solution.py:126
  102.5 2.1 select_convert_fusion.15
  108.8 8.3 %conv3x3_rows.13 = f32[2,4,320,128]{3,2,1,0:T(8,128)} custom-call(bf16[3,2,6,320,128]{4,3,2,1,0:T(8,128)(2,1)} %pad_maximum_fusion.5.x_ref, bf16[1,2,9,320,320]{4,3,2,1,0:T(8,128)(2,1)} %w_ref.7), custom_call_target="tpu_custom_call" | custom-call | flops 1887436800 | bytes 6103040 | tf_op jit(solution)/shard_map/conv3x3_rows/pallas_call | solution.py:272
  118.8 65.6 %conditional.5 = (bf16[2,4,320,128]{3,2,1,0:T(8,128)(2,1)S(1)}) conditional(s32[]{:T(128)} %bitcast.122, bf16[2,4,320,128]{3,2,1,0:T(8,128)(2,1)S(1)} %add_convert_fusion.3, (bf16[2,4,320,128]{3,2,1,0:T(8,128)(2,1)S(1)}, f32[1,2,2,320]{3,2,1,0:T(2,128)S(1)}, f32[1,2,2,320]{3,2,1,0:T(2,128)S(1)}, bf16[1,2,9,320,320]{4,3,2,1,0:T(8,128)(2,1)}, ...), branch_computations={%region_23.24_spmd, %region_24.39_spmd} | conditional | flops 3809128960 | bytes 63341760 | solution.py:361
  121.6 10.3 %exchange_stats_rows.11 = (f32[16,8,128]{2,1,0:T(8,128)}, bf16[2,320,128]{2,1,0:T(8,128)(2,1)}, bf16[2,320,128]{2,1,0:T(8,128)(2,1)}) custom-call(f32[8,128]{1,0:T(8,128)} %scatter.20.refs_0_, bf16[2,320,128]{2,1,0:T(8,128)(2,1)} %get-tuple-element.303.refs_1_, bf16[2,320,128]{2,1,0:T(8,128)(2,1)} %get-tuple-element.302.refs_2_), custom_call_target="tpu_custom_call" | custom-call | tf_op jit(solution)/shard_map/cond/branch_1_fun/exchange_stats_rows/pallas_call | solution.py:126
  139.8 8.3 %conv3x3_rows.8 = f32[2,4,320,128]{3,2,1,0:T(8,128)} custom-call(bf16[3,2,6,320,128]{4,3,2,1,0:T(8,128)(2,1)} %pad_maximum_fusion.x_ref, bf16[1,2,9,320,320]{4,3,2,1,0:T(8,128)(2,1)} %get-tuple-element.183.w_ref), custom_call_target="tpu_custom_call" | custom-call | flops 1887436800 | bytes 6103040 | tf_op jit(solution)/shard_map/cond/branch_1_fun/conv3x3_rows/pallas_call | solution.py:272
  152.4 14.4 %exchange_stats_rows.12 = (f32[16,8,128]{2,1,0:T(8,128)}, f32[2,320,128]{2,1,0:T(8,128)}, f32[2,320,128]{2,1,0:T(8,128)}) custom-call(f32[8,128]{1,0:T(8,128)} %scatter.21.refs_0_, f32[2,320,128]{2,1,0:T(8,128)} %get-tuple-element.295.refs_1_, f32[2,320,128]{2,1,0:T(8,128)} %get-tuple-element.294.refs_2_), custom_call_target="tpu_custom_call" | custom-call | tf_op jit(solution)/shard_map/cond/branch_1_fun/exchange_stats_rows/pallas_call | solution.py:126
  168.4 2.1 select_convert_fusion.2
  174.3 8.3 %conv3x3_rows.9 = f32[2,4,320,128]{3,2,1,0:T(8,128)} custom-call(bf16[3,2,6,320,128]{4,3,2,1,0:T(8,128)(2,1)} %pad_maximum_fusion.1.x_ref, bf16[1,2,9,320,320]{4,3,2,1,0:T(8,128)(2,1)} %get-tuple-element.187.w_ref), custom_call_target="tpu_custom_call" | custom-call | flops 1887436800 | bytes 6103040 | tf_op jit(solution)/shard_map/cond/branch_1_fun/conv3x3_rows/pallas_call | solution.py:272
  186.6 7.9 %collective-permute-done.4 = bf16[2,4,4,128]{3,1,2,0:T(4,128)(2,1)S(1)} collective-permute-done((bf16[2,4,4,128]{3,1,2,0:T(4,128)(2,1)S(1)}, bf16[2,4,4,128]{3,1,2,0:T(4,128)(2,1)S(1)}, u32[]{:S(2)}, u32[]{:S(2)}) %collective-permute-start.4) | collective-permute-done | bytes 8224 | tf_op jit(solution)/shard_map/ppermute | solution.py:355
  196.5 4.5 %collective-permute-start.6 = (bf16[2,1,4,128]{3,2,1,0:T(4,128)(2,1)S(1)}, bf16[2,1,4,128]{3,2,1,0:T(4,128)(2,1)S(1)}, u32[]{:S(2)}, u32[]{:S(2)}) collective-permute-start(bf16[2,1,4,128]{3,2,1,0:T(4,128)(2,1)S(1)} %get-tuple-element.359), channel_id=1, source_target_pairs={{1,0},{2,1},{3,2},{4,3},{5,4},{6,5},{7,6},{8,7},{9,8},{10,9},{11,1... | collective-permute-start | bytes 6152 | tf_op jit(solution)/shard_map/ppermute | solution.py:27
  205.5 9.1 %collective-permute-done.7 = bf16[2,4,320,128]{3,2,1,0:T(8,128)(2,1)S(1)} collective-permute-done((bf16[2,4,320,128]{3,2,1,0:T(8,128)(2,1)S(1)}, bf16[2,4,320,128]{3,2,1,0:T(8,128)(2,1)S(1)}, u32[]{:S(2)}, u32[]{:S(2)}) %collective-permute-start.7) | collective-permute-done | bytes 655392 | tf_op jit(solution)/shard_map/ppermute | solution.py:35
  217.7 10.8 %exchange_stats_rows.18 = (f32[16,8,128]{2,1,0:T(8,128)}, bf16[2,320,128]{2,1,0:T(8,128)(2,1)}, bf16[2,320,128]{2,1,0:T(8,128)(2,1)}) custom-call(f32[8,128]{1,0:T(8,128)} %scatter.40.refs_0_, bf16[2,320,128]{2,1,0:T(8,128)(2,1)} %get-tuple-element.345.refs_1_, bf16[2,320,128]{2,1,0:T(8,128)(2,1)} %get-tuple-element.344.refs_2_), custom_call_target="tpu_custom_call" | custom-call | tf_op jit(solution)/shard_map/exchange_stats_rows/pallas_call | solution.py:126
  237.7 8.3 %conv3x3_rows.14 = f32[2,4,320,128]{3,2,1,0:T(8,128)} custom-call(bf16[3,2,6,320,128]{4,3,2,1,0:T(8,128)(2,1)} %pad_maximum_fusion.6.x_ref, bf16[1,2,9,320,320]{4,3,2,1,0:T(8,128)(2,1)} %w_ref.6), custom_call_target="tpu_custom_call" | custom-call | flops 1887436800 | bytes 6103040 | tf_op jit(solution)/shard_map/conv3x3_rows/pallas_call | solution.py:272
  247.9 1.9 slice_bitcast_fusion.14
  251.3 14.6 %exchange_stats_rows.19 = (f32[16,8,128]{2,1,0:T(8,128)}, f32[2,320,128]{2,1,0:T(8,128)}, f32[2,320,128]{2,1,0:T(8,128)}) custom-call(f32[8,128]{1,0:T(8,128)} %scatter.43.refs_0_, f32[2,320,128]{2,1,0:T(8,128)} %get-tuple-element.331.refs_1_, f32[2,320,128]{2,1,0:T(8,128)} %get-tuple-element.330.refs_2_), custom_call_target="tpu_custom_call" | custom-call | tf_op jit(solution)/shard_map/exchange_stats_rows/pallas_call | solution.py:126
  267.5 2.1 select_convert_fusion.11
  273.8 8.3 %conv3x3_rows.15 = f32[2,4,320,128]{3,2,1,0:T(8,128)} custom-call(bf16[3,2,6,320,128]{4,3,2,1,0:T(8,128)(2,1)} %pad_maximum_fusion.7.x_ref, bf16[1,2,9,320,320]{4,3,2,1,0:T(8,128)(2,1)} %w_ref.7), custom_call_target="tpu_custom_call" | custom-call | flops 1887436800 | bytes 6103040 | tf_op jit(solution)/shard_map/conv3x3_rows/pallas_call | solution.py:272
  283.7 65.7 %conditional.7 = (bf16[2,4,320,128]{3,2,1,0:T(8,128)(2,1)S(1)}) conditional(s32[]{:T(128)} %bitcast.122, bf16[2,4,320,128]{3,2,1,0:T(8,128)(2,1)S(1)} %add_convert_fusion.2, (bf16[2,4,320,128]{3,2,1,0:T(8,128)(2,1)S(1)}, f32[1,2,2,320]{3,2,1,0:T(2,128)S(1)}, f32[1,2,2,320]{3,2,1,0:T(2,128)S(1)}, bf16[1,2,9,320,320]{4,3,2,1,0:T(8,128)(2,1)}, ...), branch_computations={%region_62.63_spmd, %region_63.78_spmd} | conditional | flops 3809128960 | bytes 63341760 | solution.py:361
  286.5 10.5 %exchange_stats_rows.14 = (f32[16,8,128]{2,1,0:T(8,128)}, bf16[2,320,128]{2,1,0:T(8,128)(2,1)}, bf16[2,320,128]{2,1,0:T(8,128)(2,1)}) custom-call(f32[8,128]{1,0:T(8,128)} %scatter.25.refs_0_, bf16[2,320,128]{2,1,0:T(8,128)(2,1)} %get-tuple-element.321.refs_1_, bf16[2,320,128]{2,1,0:T(8,128)(2,1)} %get-tuple-element.320.refs_2_), custom_call_target="tpu_custom_call" | custom-call | tf_op jit(solution)/shard_map/cond/branch_1_fun/exchange_stats_rows/pallas_call | solution.py:126
  304.9 8.3 %conv3x3_rows.10 = f32[2,4,320,128]{3,2,1,0:T(8,128)} custom-call(bf16[3,2,6,320,128]{4,3,2,1,0:T(8,128)(2,1)} %pad_maximum_fusion.2.x_ref, bf16[1,2,9,320,320]{4,3,2,1,0:T(8,128)(2,1)} %get-tuple-element.201.w_ref), custom_call_target="tpu_custom_call" | custom-call | flops 1887436800 | bytes 6103040 | tf_op jit(solution)/shard_map/cond/branch_1_fun/conv3x3_rows/pallas_call | solution.py:272
  317.5 14.3 %exchange_stats_rows.15 = (f32[16,8,128]{2,1,0:T(8,128)}, f32[2,320,128]{2,1,0:T(8,128)}, f32[2,320,128]{2,1,0:T(8,128)}) custom-call(f32[8,128]{1,0:T(8,128)} %scatter.28.refs_0_, f32[2,320,128]{2,1,0:T(8,128)} %get-tuple-element.313.refs_1_, f32[2,320,128]{2,1,0:T(8,128)} %get-tuple-element.312.refs_2_), custom_call_target="tpu_custom_call" | custom-call | tf_op jit(solution)/shard_map/cond/branch_1_fun/exchange_stats_rows/pallas_call | solution.py:126
  333.4 2.1 select_convert_fusion.6
  339.3 8.3 %conv3x3_rows.11 = f32[2,4,320,128]{3,2,1,0:T(8,128)} custom-call(bf16[3,2,6,320,128]{4,3,2,1,0:T(8,128)(2,1)} %pad_maximum_fusion.3.x_ref, bf16[1,2,9,320,320]{4,3,2,1,0:T(8,128)(2,1)} %get-tuple-element.205.w_ref), custom_call_target="tpu_custom_call" | custom-call | flops 1887436800 | bytes 6103040 | tf_op jit(solution)/shard_map/cond/branch_1_fun/conv3x3_rows/pallas_call | solution.py:272
  350.4 10.6 %scatter_latent_columns.1 = f32[4,128]{1,0:T(4,128)} custom-call(f32[8,4,128]{2,1,0:T(4,128)} %reshape.1722.refs_0_), custom_call_target="tpu_custom_call" | custom-call | tf_op jit(solution)/shard_map/scatter_latent_columns/pallas_call | solution.py:230
  (352 shorter events, 108.5 us)
Async XLA Ops:
  2.6 48.2 %collective-permute-start.3 = (bf16[2,4,320,128]{3,2,1,0:T(8,128)(2,1)}, bf16[2,4,320,128]{3,2,1,0:T(8,128)(2,1)S(1)}, u32[]{:S(2)}, u32[]{:S(2)}) collective-permute-start(bf16[2,4,320,128]{3,2,1,0:T(8,128)(2,1)} %bitcast.472), channel_id=1, source_target_pairs={{0,16},{16,32},{32,48},{48,64},{64,80},{80,96},{96,112},{1,17},{17... | collective-permute-start | bytes 1966088 | tf_op jit(solution)/shard_map/ppermute | solution.py:35
  7.5 2.1 copy-start.21
  7.5 2.1 copy-start.23
  7.5 40.2 %copy-start.18 = (bf16[9,320,4]{1,2,0:T(4,128)(2,1)S(1)}, bf16[9,320,4]{1,2,0:T(4,128)(2,1)}, u32[]{:S(2)}) copy-start(bf16[9,320,4]{1,2,0:T(4,128)(2,1)} %param.48) | copy-start | bytes 69124
  8.3 31.6 %collective-permute-start = (bf16[2,4,4,128]{3,1,2,0:T(4,128)(2,1)S(1)}, bf16[2,4,4,128]{3,1,2,0:T(4,128)(2,1)S(1)}, u32[]{:S(2)}, u32[]{:S(2)}) collective-permute-start(bf16[2,4,4,128]{3,1,2,0:T(4,128)(2,1)S(1)} %divide_convert_fusion.1), channel_id=1, source_target_pairs={{112,0},{113,1},{114,2},{115,3},{116,4},{117,5},{118,6},{119,7},{1... | collective-permute-start | bytes 24584 | tf_op jit(solution)/shard_map/ppermute | solution.py:355
  39.9 7.1 %collective-permute-start.1 = (bf16[2,1,4,128]{3,2,1,0:T(4,128)(2,1)S(1)}, bf16[2,1,4,128]{3,2,1,0:T(4,128)(2,1)S(1)}, u32[]{:S(2)}, u32[]{:S(2)}) collective-permute-start(bf16[2,1,4,128]{3,2,1,0:T(4,128)(2,1)S(1)} %get-tuple-element.360), channel_id=1, source_target_pairs={{0,1},{1,2},{2,3},{3,4},{4,5},{5,6},{6,7},{7,8},{8,9},{9,10},{10,1... | collective-permute-start | bytes 6152 | tf_op jit(solution)/shard_map/ppermute | solution.py:24
  41.8 5.8 %collective-permute-start.2 = (bf16[2,1,4,128]{3,2,1,0:T(4,128)(2,1)S(1)}, bf16[2,1,4,128]{3,2,1,0:T(4,128)(2,1)S(1)}, u32[]{:S(2)}, u32[]{:S(2)}) collective-permute-start(bf16[2,1,4,128]{3,2,1,0:T(4,128)(2,1)S(1)} %get-tuple-element.361), channel_id=1, source_target_pairs={{1,0},{2,1},{3,2},{4,3},{5,4},{6,5},{7,6},{8,7},{9,8},{10,9},{11,1... | collective-permute-start | bytes 6152 | tf_op jit(solution)/shard_map/ppermute | solution.py:27
  64.8 1.8 copy-start.13
  80.9 4.0 %copy-start.1 = (f32[2,4,320,128]{3,2,1,0:T(8,128)S(1)}, f32[2,4,320,128]{3,2,1,0:T(8,128)}, u32[]{:S(2)}) copy-start(f32[2,4,320,128]{3,2,1,0:T(8,128)} %conv3x3_rows.12) | copy-start | bytes 3932164
  104.7 1.0 copy-start.5
  104.7 1.1 copy-start.6
  117.2 1.6 copy-start.22
  117.2 1.6 copy-start.24
  118.8 65.6 %copy-start.16 = (bf16[9,4,320]{2,1,0:T(4,128)(2,1)S(1)}, bf16[9,4,320]{2,1,0:T(4,128)(2,1)}, u32[]{:S(2)}) copy-start(bf16[9,4,320]{2,1,0:T(4,128)(2,1)} %param.49) | copy-start | bytes 69124
  118.8 65.6 %copy-start.25 = (f32[320]{0:T(512)S(1)}, f32[320]{0:T(512)}, u32[]{:S(2)}) copy-start(f32[320]{0:T(512)} %param.50) | copy-start | bytes 3844
  118.8 65.6 %copy-start.27 = (f32[320]{0:T(512)S(1)}, f32[320]{0:T(512)}, u32[]{:S(2)}) copy-start(f32[320]{0:T(512)} %param.51) | copy-start | bytes 3844
  148.2 2.1 copy-start.2
  166.8 3.8 %copy-start.9 = (f32[2,320,128]{2,1,0:T(8,128)S(1)}, f32[2,320,128]{2,1,0:T(8,128)}, u32[]{:S(2)}) copy-start(f32[2,320,128]{2,1,0:T(8,128)} %get-tuple-element.184) | copy-start | bytes 983044 | tf_op jit(solution)/shard_map/cond
  166.8 3.8 %copy-start.10 = (f32[2,320,128]{2,1,0:T(8,128)S(1)}, f32[2,320,128]{2,1,0:T(8,128)}, u32[]{:S(2)}) copy-start(f32[2,320,128]{2,1,0:T(8,128)} %get-tuple-element.185) | copy-start | bytes 983044 | tf_op jit(solution)/shard_map/cond
  185.3 9.2 %collective-permute-start.4 = (bf16[2,4,4,128]{3,1,2,0:T(4,128)(2,1)S(1)}, bf16[2,4,4,128]{3,1,2,0:T(4,128)(2,1)S(1)}, u32[]{:S(2)}, u32[]{:S(2)}) collective-permute-start(bf16[2,4,4,128]{3,1,2,0:T(4,128)(2,1)S(1)} %get-tuple-element.284), channel_id=1, source_target_pairs={{112,0},{113,1},{114,2},{115,3},{116,4},{117,5},{118,6},{119,7},{1... | collective-permute-start | bytes 24584 | tf_op jit(solution)/shard_map/ppermute | solution.py:355
  194.5 7.8 %collective-permute-start.5 = (bf16[2,1,4,128]{3,2,1,0:T(4,128)(2,1)S(1)}, bf16[2,1,4,128]{3,2,1,0:T(4,128)(2,1)S(1)}, u32[]{:S(2)}, u32[]{:S(2)}) collective-permute-start(bf16[2,1,4,128]{3,2,1,0:T(4,128)(2,1)S(1)} %get-tuple-element.358), channel_id=1, source_target_pairs={{0,1},{1,2},{2,3},{3,4},{4,5},{5,6},{6,7},{7,8},{8,9},{9,10},{10,1... | collective-permute-start | bytes 6152 | tf_op jit(solution)/shard_map/ppermute | solution.py:24
  196.5 5.9 %collective-permute-start.6 = (bf16[2,1,4,128]{3,2,1,0:T(4,128)(2,1)S(1)}, bf16[2,1,4,128]{3,2,1,0:T(4,128)(2,1)S(1)}, u32[]{:S(2)}, u32[]{:S(2)}) collective-permute-start(bf16[2,1,4,128]{3,2,1,0:T(4,128)(2,1)S(1)} %get-tuple-element.359), channel_id=1, source_target_pairs={{1,0},{2,1},{3,2},{4,3},{5,4},{6,5},{7,6},{8,7},{9,8},{10,9},{11,1... | collective-permute-start | bytes 6152 | tf_op jit(solution)/shard_map/ppermute | solution.py:27
  201.0 13.6 %collective-permute-start.7 = (bf16[2,4,320,128]{3,2,1,0:T(8,128)(2,1)S(1)}, bf16[2,4,320,128]{3,2,1,0:T(8,128)(2,1)S(1)}, u32[]{:S(2)}, u32[]{:S(2)}) collective-permute-start(bf16[2,4,320,128]{3,2,1,0:T(8,128)(2,1)S(1)} %get-tuple-element.375), channel_id=1, source_target_pairs={{0,16},{16,32},{32,48},{48,64},{64,80},{80,96},{96,112},{1,17},{17... | collective-permute-start | bytes 1966088 | tf_op jit(solution)/shard_map/ppermute | solution.py:35
  228.6 2.9 copy-start.15
  229.7 1.9 copy-start.14
  231.5 1.3 copy-start.4
  246.0 4.0 %copy-start = (f32[2,4,320,128]{3,2,1,0:T(8,128)S(1)}, f32[2,4,320,128]{3,2,1,0:T(8,128)}, u32[]{:S(2)}) copy-start(f32[2,4,320,128]{3,2,1,0:T(8,128)} %conv3x3_rows.14) | copy-start | bytes 3932164
  269.7 1.0 copy-start.7
  269.7 1.1 copy-start.8
  313.2 2.1 copy-start.3
  331.8 3.8 %copy-start.11 = (f32[2,320,128]{2,1,0:T(8,128)S(1)}, f32[2,320,128]{2,1,0:T(8,128)}, u32[]{:S(2)}) copy-start(f32[2,320,128]{2,1,0:T(8,128)} %get-tuple-element.202) | copy-start | bytes 983044 | tf_op jit(solution)/shard_map/cond
  331.8 3.8 %copy-start.12 = (f32[2,320,128]{2,1,0:T(8,128)S(1)}, f32[2,320,128]{2,1,0:T(8,128)}, u32[]{:S(2)}) copy-start(f32[2,320,128]{2,1,0:T(8,128)} %get-tuple-element.203) | copy-start | bytes 983044 | tf_op jit(solution)/shard_map/cond
  (6 other events, 4.1 us)
